TPU v7x, 256 devices: a whole 4x4x8 slice. The times are simulated.
256 devices in a mesh: sub: 32 (over x, z), col: 8 (over y, core).
Axes of the slice: x: 4, y: 4, z: 8, core: 2. Of those that a mesh axis runs over, the one named last changes fastest.
Arguments:
- trace_start: bfloat16 [32, 8, 1536, 128], P('sub', 'col'), may hold values from -6 to 6
- neumann_load: bfloat16 [32, 8, 1536, 128], P('sub', 'col'), may hold values from -6 to 6
- double_layer: bfloat16 [32, 8, 1536, 1536], P('sub', 'col'), may hold values from -0.15625 to 0.15625
- single_inverse: bfloat16 [32, 8, 1536, 1536], P('sub', 'col'), may hold values from -0.15625 to 0.15625
- interface_nodes: int32 [32, 8, 8, 128], P('sub', 'col'), may hold values from -1 to 1023, as said below
- node_mode: int32 [32, 8, 1536], P('sub', 'col'), may hold values from 0 to 63
- mode_weight: bfloat16 [32, 8, 1536], P('sub', 'col'), may hold values from 0.5 to 1.5
- coarse_inverse: bfloat16 [16384, 16384], P('sub', 'col'), may hold values from -0.005859375 to 0.005859375
Outputs:
- final_trace: bfloat16 [32, 8, 1536, 128], P('sub', 'col')
- final_residual: bfloat16 [32, 8, 1536, 128], P('sub', 'col')
Inputs may be any that keep to these rules, and one draw needn't show every extreme that they name: `interface_nodes`: entry k of block (s, d) is a boundary node of s, within nodes d * 128 to (d + 1) * 128 - 1, distinct within the block, and matches entry k of the neighbour's block for direction 7 - d; valid entries come first and the rest are -1; blocks toward outside the grid are all -1; blocks of directions 1, 3, 4, 6 have 128 / 2 to 128 valid entries, the others 1 to 16, and some block has 128.
All inputs are finite; a program needn't handle non-finite values.
Results may differ from a plain program's by a relative error of at most 0.019.
Values may be sent and summed in bfloat16 or wider, within the bound.
A program may use at most 64 MiB of HBM per device.

v0:
```python
import jax
import jax.numpy as jnp
from jax import lax
from jax.sharding import PartitionSpec as P

MODES = 64
ITERS = 3
DIRECTIONS = ((-1, -1), (-1, 0), (-1, 1), (0, -1), (0, 1), (1, -1), (1, 0), (1, 1))


def from_behind(value, axis, by):
    devices = lax.axis_size(axis)
    pairs = [(i, i + by) for i in range(devices) if 0 <= i + by < devices]
    return lax.ppermute(value, axis, pairs)


def deliver_single(outgoing):
    arrivals = []
    for toward in range(8):
        row_step, col_step = DIRECTIONS[toward]
        message = outgoing[7 - toward]
        if row_step != 0:
            message = from_behind(message, "sub", -row_step)
        if col_step != 0:
            message = from_behind(message, "col", -col_step)
        arrivals.append(message)
    return jnp.stack(arrivals)


def local(
    trace_start,
    neumann_load,
    double_layer,
    single_inverse,
    interface_nodes,
    node_mode,
    mode_weight,
    coarse_inverse,
):
    trace_now = trace_start[0, 0]
    load_block = neumann_load[0, 0].astype(jnp.float32)
    kernel = double_layer[0, 0]
    inverse = single_inverse[0, 0]
    node_count = kernel.shape[0]
    interface = interface_nodes[0, 0]
    slot_count = interface.shape[1]
    band_rows = 8 * slot_count
    local_index = interface - (jnp.arange(8, dtype=jnp.int32) * slot_count)[:, None]
    selector = (
        local_index[:, :, None] == jnp.arange(slot_count, dtype=jnp.int32)[None, None, :]
    ).astype(jnp.bfloat16)
    mode_basis = jnp.where(
        node_mode[0, 0][None, :] == jnp.arange(MODES, dtype=jnp.int32)[:, None],
        mode_weight[0, 0][None, :],
        jnp.zeros((), jnp.bfloat16),
    )
    rhs_count = trace_now.shape[1]
    residual = trace_now
    rest_zeros = jnp.zeros((node_count - band_rows, rhs_count), jnp.float32)
    for iteration in range(ITERS):
        mixed_trace = (
            0.5 * trace_now.astype(jnp.float32)
            + jnp.dot(kernel, trace_now, preferred_element_type=jnp.float32)
        ).astype(jnp.bfloat16)
        flux_now = jnp.dot(inverse, mixed_trace, preferred_element_type=jnp.float32).astype(
            jnp.bfloat16
        )
        banded = flux_now[:band_rows].reshape(8, slot_count, rhs_count)
        outgoing = jnp.einsum(
            "dpq,dqr->dpr", selector, banded, preferred_element_type=jnp.float32
        ).astype(jnp.bfloat16)
        received = deliver_single(outgoing)
        placed = jnp.einsum(
            "dpq,dpr->dqr", selector, received, preferred_element_type=jnp.float32
        ).reshape(band_rows, rhs_count)
        assembled = flux_now.astype(jnp.float32) + jnp.concatenate([placed, rest_zeros], axis=0)
        residual = (load_block - assembled).astype(jnp.bfloat16)
        residual = lax.optimization_barrier(residual)
        coarse_rhs = jnp.dot(mode_basis, residual, preferred_element_type=jnp.float32).astype(
            jnp.bfloat16
        )
        partial_value = jnp.dot(
            coarse_inverse,
            lax.all_gather(coarse_rhs, "sub", axis=0, tiled=True),
            preferred_element_type=jnp.float32,
        )
        coarse_out = lax.psum_scatter(
            partial_value.astype(jnp.bfloat16), "col", scatter_dimension=0, tiled=True
        )
        correction = lax.dot_general(
            mode_basis, coarse_out, (((0,), (0,)), ((), ())), preferred_element_type=jnp.float32
        )
        trace_now = (
            trace_now.astype(jnp.float32) + 0.25 * residual.astype(jnp.float32) + correction
        ).astype(jnp.bfloat16)
    return (trace_now[None, None], residual[None, None])


def solution(mesh):
    placed = (
        P("sub", "col", None, None),
        P("sub", "col", None, None),
        P("sub", "col", None, None),
        P("sub", "col", None, None),
        P("sub", "col", None, None),
        P("sub", "col", None),
        P("sub", "col", None),
        P("sub", "col"),
    )
    return jax.shard_map(
        local,
        mesh=mesh,
        in_specs=placed,
        out_specs=(P("sub", "col", None, None), P("sub", "col", None, None)),
        check_vma=False,
    )
```

profile of v0, /device:TPU:2, one launch (start us, length us, event | category | flops | bytes accessed | tf_op | source)
XLA Modules:
  0.0 430.3 jit_solution(12199868396667985276)
XLA Ops:
  7.2 1.3 copy.26
  8.6 7.1 %fusion.54 = bf16[1536,128]{0,1:T(8,128)(2,1)S(1)} fusion(bf16[1,1,1536,1536]{3,2,1,0:T(8,128)(2,1)} %param.11, bf16[1,1,1536,1536]{3,2,1,0:T(8,128)(2,1)} %param.10, bf16[1,1,1536,128]{3,2,1,0:T(8,128)(2,1)} %param.8, bf16[1,1,1536,128]{2,3,1,0:T(8,128)(2,1)S(1)} %copy.26), kind=kOutput, calls=%fused_computation.31 | convolution fusion | flops 1208942592 | bytes 10616832 | tf_op jit(solution)/shard_map/dot_general | solution.py:65
  16.3 3.8 collective-permute-start
  20.2 5.9 %collective-permute-done = bf16[128,128]{1,0:T(8,128)(2,1)} collective-permute-done((bf16[128,128]{1,0:T(8,128)(2,1)S(1)}, bf16[128,128]{1,0:T(8,128)(2,1)}, u32[]{:S(2)}, u32[]{:S(2)}) %collective-permute-start) | collective-permute-done | bytes 32800 | tf_op jit(solution)/shard_map/ppermute | solution.py:14
  26.1 1.9 collective-permute-start.1
  27.9 3.9 collective-permute-start.10
  31.8 2.9 collective-permute-start.9
  34.8 2.9 collective-permute-start.7
  37.7 2.9 collective-permute-start.3
  40.6 1.2 copy.27
  42.6 2.9 collective-permute-start.2
  46.3 1.3 collective-permute-start.6
  47.6 2.9 collective-permute-done.2
  50.5 1.3 collective-permute-start.4
  51.8 3.0 collective-permute-start.5
  54.9 1.3 collective-permute-start.11
  56.2 3.8 collective-permute-start.8
  62.1 2.1 copy.49
  64.1 1.2 fusion.61
  66.3 47.7 %all_gather.9 = bf16[2048,128]{1,0:T(8,128)(2,1)S(1)} all-gather(bf16[64,128]{1,0:T(8,128)(2,1)S(1)} %convolution_convert_fusion.8), channel_id=1, replica_groups=mesh['sub'=32,'col'=8] {'sub'}, dimensions={0}, use_global_device_ids=true | all-gather | bytes 540672 | tf_op jit(solution)/shard_map/all_gather | solution.py:84
  115.7 33.5 %reduce-scatter.10.cloned.1.call-done = bf16[64,128]{1,0:T(8,128)(2,1)} async-done(((bf16[512,128]{1,0:T(8,128)(2,1)}), bf16[64,128]{1,0:T(8,128)(2,1)}) %reduce-scatter.10.cloned.1.call-update) | async-done | bytes 16400
  149.2 1.3 fusion.27
  150.5 6.9 %fusion.51 = bf16[1536,128]{0,1:T(8,128)(2,1)S(1)} fusion(bf16[1,1,1536,1536]{3,2,1,0:T(8,128)(2,1)} %param.11, bf16[1536,128]{0,1:T(8,128)(2,1)S(1)} %fusion.27, bf16[1,1,1536,1536]{3,2,1,0:T(8,128)(2,1)} %param.10), kind=kOutput, calls=%fused_computation.30 | convolution fusion | flops 1208942592 | bytes 10223616 | tf_op jit(solution)/shard_map/dot_general | solution.py:65
  158.2 1.1 copy.50
  159.7 3.5 collective-permute-start.12
  163.2 4.4 %collective-permute-done.12 = bf16[128,128]{1,0:T(8,128)(2,1)S(1)} collective-permute-done((bf16[128,128]{1,0:T(8,128)(2,1)S(1)}, bf16[128,128]{1,0:T(8,128)(2,1)S(1)}, u32[]{:S(2)}, u32[]{:S(2)}) %collective-permute-start.12) | collective-permute-done | bytes 32800 | tf_op jit(solution)/shard_map/ppermute | solution.py:14
  167.6 1.3 collective-permute-start.13
  168.9 3.1 collective-permute-start.22
  172.0 3.3 collective-permute-start.21
  175.3 3.3 collective-permute-start.19
  178.6 2.6 collective-permute-start.15
  181.2 2.6 collective-permute-start.14
  183.8 2.9 collective-permute-done.15
  186.6 1.3 collective-permute-start.18
  187.9 1.1 collective-permute-done.14
  189.1 1.3 collective-permute-start.16
  190.4 3.0 collective-permute-start.17
  193.4 1.3 collective-permute-start.23
  194.7 3.8 collective-permute-start.20
  200.4 2.1 copy.51
  202.5 1.2 fusion.62
  204.7 47.6 %all_gather.10 = bf16[2048,128]{1,0:T(8,128)(2,1)S(1)} all-gather(bf16[64,128]{1,0:T(8,128)(2,1)S(1)} %convolution_convert_fusion.7), channel_id=1, replica_groups=mesh['sub'=32,'col'=8] {'sub'}, dimensions={0}, use_global_device_ids=true | all-gather | bytes 540672 | tf_op jit(solution)/shard_map/all_gather | solution.py:84
  254.1 31.7 %reduce-scatter.12.cloned.1.call-done = bf16[64,128]{1,0:T(8,128)(2,1)} async-done(((bf16[512,128]{1,0:T(8,128)(2,1)}), bf16[64,128]{1,0:T(8,128)(2,1)}) %reduce-scatter.12.cloned.1.call-update) | async-done | bytes 16400
  285.8 1.3 fusion.28
  287.1 6.9 %fusion.48 = bf16[1536,128]{0,1:T(8,128)(2,1)S(1)} fusion(bf16[1,1,1536,1536]{3,2,1,0:T(8,128)(2,1)} %param.11, bf16[1536,128]{0,1:T(8,128)(2,1)S(1)} %fusion.28, bf16[1,1,1536,1536]{3,2,1,0:T(8,128)(2,1)} %param.10), kind=kOutput, calls=%fused_computation.29 | convolution fusion | flops 1208942592 | bytes 10223616 | tf_op jit(solution)/shard_map/dot_general | solution.py:65
  296.4 3.5 collective-permute-start.24
  299.8 4.5 %collective-permute-done.24 = bf16[128,128]{1,0:T(8,128)(2,1)S(1)} collective-permute-done((bf16[128,128]{1,0:T(8,128)(2,1)S(1)}, bf16[128,128]{1,0:T(8,128)(2,1)S(1)}, u32[]{:S(2)}, u32[]{:S(2)}) %collective-permute-start.24) | collective-permute-done | bytes 32800 | tf_op jit(solution)/shard_map/ppermute | solution.py:14
  304.3 1.3 collective-permute-start.25
  305.6 3.0 collective-permute-start.34
  308.6 3.4 collective-permute-start.33
  312.0 3.2 collective-permute-start.31
  315.2 2.6 collective-permute-start.27
  317.8 2.5 collective-permute-start.26
  320.3 3.0 collective-permute-done.27
  323.3 1.3 collective-permute-start.30
  324.6 1.2 collective-permute-done.26
  325.7 1.3 collective-permute-start.28
  327.1 3.0 collective-permute-start.29
  330.1 1.3 collective-permute-start.35
  331.4 3.8 collective-permute-start.32
  337.1 2.1 copy.53
  339.2 1.3 fusion.63
  340.7 47.7 %all_gather.11 = bf16[2048,128]{1,0:T(8,128)(2,1)S(1)} all-gather(bf16[64,128]{1,0:T(8,128)(2,1)S(1)} %convolution_convert_fusion.6), channel_id=1, replica_groups=mesh['sub'=32,'col'=8] {'sub'}, dimensions={0}, use_global_device_ids=true | all-gather | bytes 540672 | tf_op jit(solution)/shard_map/all_gather | solution.py:84
  390.9 31.0 %reduce-scatter.14.cloned.1.call-done = bf16[64,128]{1,0:T(8,128)(2,1)} async-done(((bf16[512,128]{1,0:T(8,128)(2,1)}), bf16[64,128]{1,0:T(8,128)(2,1)}) %reduce-scatter.14.cloned.1.call-update) | async-done | bytes 16400
  (100 shorter events, 21.6 us)
Async XLA Ops:
  7.2 106.8 %copy-start = (bf16[512,2048]{1,0:T(8,128)(2,1)S(1)}, bf16[512,2048]{1,0:T(8,128)(2,1)}, u32[]{:S(2)}) copy-start(bf16[512,2048]{1,0:T(8,128)(2,1)} %param.15) | copy-start | bytes 6291460
  7.2 142.0 %reduce-scatter.10.cloned.1.call-start = ((), (), s32[]{:S(2)}) async-start(), calls=%async_computation.3 | async-start | bytes 147456
  8.5 7.3 %copy-start.5 = (s32[1,1,8,128]{3,2,1,0:T(8,128)S(1)}, s32[1,1,8,128]{3,2,1,0:T(8,128)}, u32[]{:S(2)}) copy-start(s32[1,1,8,128]{3,2,1,0:T(8,128)} %param.12) | copy-start | bytes 12292
  8.6 33.2 %copy-start.4 = (bf16[1,1,1536]{2,1,0:T(2,128)(2,1)S(1)}, bf16[1,1,1536]{2,1,0:T(2,128)(2,1)}, u32[]{:S(2)}) copy-start(bf16[1,1,1536]{2,1,0:T(2,128)(2,1)} %param.14) | copy-start | bytes 9220
  16.3 9.7 %collective-permute-start = (bf16[128,128]{1,0:T(8,128)(2,1)S(1)}, bf16[128,128]{1,0:T(8,128)(2,1)}, u32[]{:S(2)}, u32[]{:S(2)}) collective-permute-start(bf16[128,128]{1,0:T(8,128)(2,1)S(1)} %get-tuple-element.29), channel_id=1, source_target_pairs={{0,8},{8,16},{16,24},{24,32},{32,40},{40,48},{48,56},{56,64},{64,7... | collective-permute-start | bytes 98312 | tf_op jit(solution)/shard_map/ppermute | solution.py:14
  26.1 16.5 %collective-permute-start.1 = (bf16[128,128]{1,0:T(8,128)(2,1)}, bf16[128,128]{1,0:T(8,128)(2,1)}, u32[]{:S(2)}, u32[]{:S(2)}) collective-permute-start(bf16[128,128]{1,0:T(8,128)(2,1)} %collective-permute-done), channel_id=1, source_target_pairs={{0,1},{1,2},{2,3},{3,4},{4,5},{5,6},{6,7},{8,9},{9,10},{10,11},{11... | collective-permute-start | bytes 98312 | tf_op jit(solution)/shard_map/ppermute | solution.py:14
  27.9 23.9 %collective-permute-start.10 = (bf16[128,128]{1,0:T(8,128)(2,1)S(1)}, bf16[128,128]{1,0:T(8,128)(2,1)}, u32[]{:S(2)}, u32[]{:S(2)}) collective-permute-start(bf16[128,128]{1,0:T(8,128)(2,1)S(1)} %get-tuple-element.22), channel_id=1, source_target_pairs={{8,0},{16,8},{24,16},{32,24},{40,32},{48,40},{56,48},{64,56},{72,6... | collective-permute-start | bytes 98312 | tf_op jit(solution)/shard_map/ppermute | solution.py:14
  31.8 29.2 %collective-permute-start.9 = (bf16[128,128]{1,0:T(8,128)(2,1)S(1)}, bf16[128,128]{1,0:T(8,128)(2,1)S(1)}, u32[]{:S(2)}, u32[]{:S(2)}) collective-permute-start(bf16[128,128]{1,0:T(8,128)(2,1)S(1)} %get-tuple-element.23), channel_id=1, source_target_pairs={{8,0},{16,8},{24,16},{32,24},{40,32},{48,40},{56,48},{64,56},{72,6... | collective-permute-start | bytes 98312 | tf_op jit(solution)/shard_map/ppermute | solution.py:14
  34.8 20.1 %collective-permute-start.7 = (bf16[128,128]{1,0:T(8,128)(2,1)S(1)}, bf16[128,128]{1,0:T(8,128)(2,1)}, u32[]{:S(2)}, u32[]{:S(2)}) collective-permute-start(bf16[128,128]{1,0:T(8,128)(2,1)S(1)} %get-tuple-element.24), channel_id=1, source_target_pairs={{8,0},{16,8},{24,16},{32,24},{40,32},{48,40},{56,48},{64,56},{72,6... | collective-permute-start | bytes 98312 | tf_op jit(solution)/shard_map/ppermute | solution.py:14
  37.7 8.6 %collective-permute-start.3 = (bf16[128,128]{1,0:T(8,128)(2,1)S(1)}, bf16[128,128]{1,0:T(8,128)(2,1)}, u32[]{:S(2)}, u32[]{:S(2)}) collective-permute-start(bf16[128,128]{1,0:T(8,128)(2,1)S(1)} %get-tuple-element.27), channel_id=1, source_target_pairs={{0,8},{8,16},{16,24},{24,32},{32,40},{40,48},{48,56},{56,64},{64,7... | collective-permute-start | bytes 98312 | tf_op jit(solution)/shard_map/ppermute | solution.py:14
  42.6 7.9 %collective-permute-start.2 = (bf16[128,128]{1,0:T(8,128)(2,1)S(1)}, bf16[128,128]{1,0:T(8,128)(2,1)S(1)}, u32[]{:S(2)}, u32[]{:S(2)}) collective-permute-start(bf16[128,128]{1,0:T(8,128)(2,1)S(1)} %get-tuple-element.28), channel_id=1, source_target_pairs={{0,8},{8,16},{16,24},{24,32},{32,40},{40,48},{48,56},{56,64},{64,7... | collective-permute-start | bytes 98312 | tf_op jit(solution)/shard_map/ppermute | solution.py:14
  46.3 13.7 %collective-permute-start.6 = (bf16[128,128]{1,0:T(8,128)(2,1)S(1)}, bf16[128,128]{1,0:T(8,128)(2,1)S(1)}, u32[]{:S(2)}, u32[]{:S(2)}) collective-permute-start(bf16[128,128]{1,0:T(8,128)(2,1)S(1)} %get-tuple-element.25), channel_id=1, source_target_pairs={{1,0},{2,1},{3,2},{4,3},{5,4},{6,5},{7,6},{9,8},{10,9},{11,10},{12... | collective-permute-start | bytes 98312 | tf_op jit(solution)/shard_map/ppermute | solution.py:14
  50.5 5.7 %collective-permute-start.4 = (bf16[128,128]{1,0:T(8,128)(2,1)}, bf16[128,128]{1,0:T(8,128)(2,1)S(1)}, u32[]{:S(2)}, u32[]{:S(2)}) collective-permute-start(bf16[128,128]{1,0:T(8,128)(2,1)} %collective-permute-done.3), channel_id=1, source_target_pairs={{1,0},{2,1},{3,2},{4,3},{5,4},{6,5},{7,6},{9,8},{10,9},{11,10},{12... | collective-permute-start | bytes 98312 | tf_op jit(solution)/shard_map/ppermute | solution.py:14
  51.8 8.2 %collective-permute-start.5 = (bf16[128,128]{1,0:T(8,128)(2,1)S(1)}, bf16[128,128]{1,0:T(8,128)(2,1)S(1)}, u32[]{:S(2)}, u32[]{:S(2)}) collective-permute-start(bf16[128,128]{1,0:T(8,128)(2,1)S(1)} %get-tuple-element.26), channel_id=1, source_target_pairs={{0,1},{1,2},{2,3},{3,4},{4,5},{5,6},{6,7},{8,9},{9,10},{10,11},{11... | collective-permute-start | bytes 98312 | tf_op jit(solution)/shard_map/ppermute | solution.py:14
  54.9 6.2 %collective-permute-start.11 = (bf16[128,128]{1,0:T(8,128)(2,1)}, bf16[128,128]{1,0:T(8,128)(2,1)S(1)}, u32[]{:S(2)}, u32[]{:S(2)}) collective-permute-start(bf16[128,128]{1,0:T(8,128)(2,1)} %collective-permute-done.10), channel_id=1, source_target_pairs={{1,0},{2,1},{3,2},{4,3},{5,4},{6,5},{7,6},{9,8},{10,9},{11,10},{12... | collective-permute-start | bytes 98312 | tf_op jit(solution)/shard_map/ppermute | solution.py:14
  56.2 4.8 %collective-permute-start.8 = (bf16[128,128]{1,0:T(8,128)(2,1)}, bf16[128,128]{1,0:T(8,128)(2,1)S(1)}, u32[]{:S(2)}, u32[]{:S(2)}) collective-permute-start(bf16[128,128]{1,0:T(8,128)(2,1)} %collective-permute-done.7), channel_id=1, source_target_pairs={{0,1},{1,2},{2,3},{3,4},{4,5},{5,6},{6,7},{8,9},{9,10},{10,11},{11... | collective-permute-start | bytes 98312 | tf_op jit(solution)/shard_map/ppermute | solution.py:14
  65.3 0.7 copy-start.2
  115.6 170.2 %reduce-scatter.12.cloned.1.call-start = ((), (), s32[]{:S(2)}) async-start(), calls=%async_computation.4 | async-start | bytes 147456
  159.7 7.9 %collective-permute-start.12 = (bf16[128,128]{1,0:T(8,128)(2,1)S(1)}, bf16[128,128]{1,0:T(8,128)(2,1)S(1)}, u32[]{:S(2)}, u32[]{:S(2)}) collective-permute-start(bf16[128,128]{1,0:T(8,128)(2,1)S(1)} %get-tuple-element.21), channel_id=1, source_target_pairs={{0,8},{8,16},{16,24},{24,32},{32,40},{40,48},{48,56},{56,64},{64,7... | collective-permute-start | bytes 98312 | tf_op jit(solution)/shard_map/ppermute | solution.py:14
  167.6 13.5 %collective-permute-start.13 = (bf16[128,128]{1,0:T(8,128)(2,1)S(1)}, bf16[128,128]{1,0:T(8,128)(2,1)S(1)}, u32[]{:S(2)}, u32[]{:S(2)}) collective-permute-start(bf16[128,128]{1,0:T(8,128)(2,1)S(1)} %collective-permute-done.12), channel_id=1, source_target_pairs={{0,1},{1,2},{2,3},{3,4},{4,5},{5,6},{6,7},{8,9},{9,10},{10,11},{11... | collective-permute-start | bytes 98312 | tf_op jit(solution)/shard_map/ppermute | solution.py:14
  168.9 21.5 %collective-permute-start.22 = (bf16[128,128]{1,0:T(8,128)(2,1)S(1)}, bf16[128,128]{1,0:T(8,128)(2,1)S(1)}, u32[]{:S(2)}, u32[]{:S(2)}) collective-permute-start(bf16[128,128]{1,0:T(8,128)(2,1)S(1)} %get-tuple-element.14), channel_id=1, source_target_pairs={{8,0},{16,8},{24,16},{32,24},{40,32},{48,40},{56,48},{64,56},{72,6... | collective-permute-start | bytes 98312 | tf_op jit(solution)/shard_map/ppermute | solution.py:14
  172.0 27.4 %collective-permute-start.21 = (bf16[128,128]{1,0:T(8,128)(2,1)S(1)}, bf16[128,128]{1,0:T(8,128)(2,1)S(1)}, u32[]{:S(2)}, u32[]{:S(2)}) collective-permute-start(bf16[128,128]{1,0:T(8,128)(2,1)S(1)} %get-tuple-element.15), channel_id=1, source_target_pairs={{8,0},{16,8},{24,16},{32,24},{40,32},{48,40},{56,48},{64,56},{72,6... | collective-permute-start | bytes 98312 | tf_op jit(solution)/shard_map/ppermute | solution.py:14
  175.3 18.1 %collective-permute-start.19 = (bf16[128,128]{1,0:T(8,128)(2,1)S(1)}, bf16[128,128]{1,0:T(8,128)(2,1)S(1)}, u32[]{:S(2)}, u32[]{:S(2)}) collective-permute-start(bf16[128,128]{1,0:T(8,128)(2,1)S(1)} %get-tuple-element.16), channel_id=1, source_target_pairs={{8,0},{16,8},{24,16},{32,24},{40,32},{48,40},{56,48},{64,56},{72,6... | collective-permute-start | bytes 98312 | tf_op jit(solution)/shard_map/ppermute | solution.py:14
  178.6 8.1 %collective-permute-start.15 = (bf16[128,128]{1,0:T(8,128)(2,1)S(1)}, bf16[128,128]{1,0:T(8,128)(2,1)S(1)}, u32[]{:S(2)}, u32[]{:S(2)}) collective-permute-start(bf16[128,128]{1,0:T(8,128)(2,1)S(1)} %get-tuple-element.19), channel_id=1, source_target_pairs={{0,8},{8,16},{16,24},{24,32},{32,40},{40,48},{48,56},{56,64},{64,7... | collective-permute-start | bytes 98312 | tf_op jit(solution)/shard_map/ppermute | solution.py:14
  181.2 7.9 %collective-permute-start.14 = (bf16[128,128]{1,0:T(8,128)(2,1)S(1)}, bf16[128,128]{1,0:T(8,128)(2,1)S(1)}, u32[]{:S(2)}, u32[]{:S(2)}) collective-permute-start(bf16[128,128]{1,0:T(8,128)(2,1)S(1)} %get-tuple-element.20), channel_id=1, source_target_pairs={{0,8},{8,16},{16,24},{24,32},{32,40},{40,48},{48,56},{56,64},{64,7... | collective-permute-start | bytes 98312 | tf_op jit(solution)/shard_map/ppermute | solution.py:14
  186.6 11.9 %collective-permute-start.18 = (bf16[128,128]{1,0:T(8,128)(2,1)S(1)}, bf16[128,128]{1,0:T(8,128)(2,1)S(1)}, u32[]{:S(2)}, u32[]{:S(2)}) collective-permute-start(bf16[128,128]{1,0:T(8,128)(2,1)S(1)} %get-tuple-element.17), channel_id=1, source_target_pairs={{1,0},{2,1},{3,2},{4,3},{5,4},{6,5},{7,6},{9,8},{10,9},{11,10},{12... | collective-permute-start | bytes 98312 | tf_op jit(solution)/shard_map/ppermute | solution.py:14
  189.1 5.7 %collective-permute-start.16 = (bf16[128,128]{1,0:T(8,128)(2,1)S(1)}, bf16[128,128]{1,0:T(8,128)(2,1)S(1)}, u32[]{:S(2)}, u32[]{:S(2)}) collective-permute-start(bf16[128,128]{1,0:T(8,128)(2,1)S(1)} %collective-permute-done.15), channel_id=1, source_target_pairs={{1,0},{2,1},{3,2},{4,3},{5,4},{6,5},{7,6},{9,8},{10,9},{11,10},{12... | collective-permute-start | bytes 98312 | tf_op jit(solution)/shard_map/ppermute | solution.py:14
  190.4 8.2 %collective-permute-start.17 = (bf16[128,128]{1,0:T(8,128)(2,1)S(1)}, bf16[128,128]{1,0:T(8,128)(2,1)S(1)}, u32[]{:S(2)}, u32[]{:S(2)}) collective-permute-start(bf16[128,128]{1,0:T(8,128)(2,1)S(1)} %get-tuple-element.18), channel_id=1, source_target_pairs={{0,1},{1,2},{2,3},{3,4},{4,5},{5,6},{6,7},{8,9},{9,10},{10,11},{11... | collective-permute-start | bytes 98312 | tf_op jit(solution)/shard_map/ppermute | solution.py:14
  193.4 6.0 %collective-permute-start.23 = (bf16[128,128]{1,0:T(8,128)(2,1)S(1)}, bf16[128,128]{1,0:T(8,128)(2,1)S(1)}, u32[]{:S(2)}, u32[]{:S(2)}) collective-permute-start(bf16[128,128]{1,0:T(8,128)(2,1)S(1)} %collective-permute-done.22), channel_id=1, source_target_pairs={{1,0},{2,1},{3,2},{4,3},{5,4},{6,5},{7,6},{9,8},{10,9},{11,10},{12... | collective-permute-start | bytes 98312 | tf_op jit(solution)/shard_map/ppermute | solution.py:14
  194.7 4.6 %collective-permute-start.20 = (bf16[128,128]{1,0:T(8,128)(2,1)S(1)}, bf16[128,128]{1,0:T(8,128)(2,1)S(1)}, u32[]{:S(2)}, u32[]{:S(2)}) collective-permute-start(bf16[128,128]{1,0:T(8,128)(2,1)S(1)} %collective-permute-done.19), channel_id=1, source_target_pairs={{0,1},{1,2},{2,3},{3,4},{4,5},{5,6},{6,7},{8,9},{9,10},{10,11},{11... | collective-permute-start | bytes 98312 | tf_op jit(solution)/shard_map/ppermute | solution.py:14
  203.7 0.7 copy-start.3
  253.9 168.0 %reduce-scatter.14.cloned.1.call-start = ((), (), s32[]{:S(2)}) async-start(), calls=%async_computation.5 | async-start | bytes 147456
  294.1 43.1 %copy-start.1 = (bf16[1536,128]{0,1:T(8,128)(2,1)}, bf16[1536,128]{0,1:T(8,128)(2,1)S(1)}, u32[]{:S(2)}) copy-start(bf16[1536,128]{0,1:T(8,128)(2,1)S(1)} %fusion.48) | copy-start | bytes 1179652
  296.4 7.9 %collective-permute-start.24 = (bf16[128,128]{1,0:T(8,128)(2,1)S(1)}, bf16[128,128]{1,0:T(8,128)(2,1)S(1)}, u32[]{:S(2)}, u32[]{:S(2)}) collective-permute-start(bf16[128,128]{1,0:T(8,128)(2,1)S(1)} %get-tuple-element.13), channel_id=1, source_target_pairs={{0,8},{8,16},{16,24},{24,32},{32,40},{40,48},{48,56},{56,64},{64,7... | collective-permute-start | bytes 98312 | tf_op jit(solution)/shard_map/ppermute | solution.py:14
  304.3 13.5 %collective-permute-start.25 = (bf16[128,128]{1,0:T(8,128)(2,1)S(1)}, bf16[128,128]{1,0:T(8,128)(2,1)S(1)}, u32[]{:S(2)}, u32[]{:S(2)}) collective-permute-start(bf16[128,128]{1,0:T(8,128)(2,1)S(1)} %collective-permute-done.24), channel_id=1, source_target_pairs={{0,1},{1,2},{2,3},{3,4},{4,5},{5,6},{6,7},{8,9},{9,10},{10,11},{11... | collective-permute-start | bytes 98312 | tf_op jit(solution)/shard_map/ppermute | solution.py:14
  305.6 21.5 %collective-permute-start.34 = (bf16[128,128]{1,0:T(8,128)(2,1)S(1)}, bf16[128,128]{1,0:T(8,128)(2,1)S(1)}, u32[]{:S(2)}, u32[]{:S(2)}) collective-permute-start(bf16[128,128]{1,0:T(8,128)(2,1)S(1)} %get-tuple-element.6), channel_id=1, source_target_pairs={{8,0},{16,8},{24,16},{32,24},{40,32},{48,40},{56,48},{64,56},{72,6... | collective-permute-start | bytes 98312 | tf_op jit(solution)/shard_map/ppermute | solution.py:14
  308.6 27.5 %collective-permute-start.33 = (bf16[128,128]{1,0:T(8,128)(2,1)S(1)}, bf16[128,128]{1,0:T(8,128)(2,1)S(1)}, u32[]{:S(2)}, u32[]{:S(2)}) collective-permute-start(bf16[128,128]{1,0:T(8,128)(2,1)S(1)} %get-tuple-element.7), channel_id=1, source_target_pairs={{8,0},{16,8},{24,16},{32,24},{40,32},{48,40},{56,48},{64,56},{72,6... | collective-permute-start | bytes 98312 | tf_op jit(solution)/shard_map/ppermute | solution.py:14
  312.0 18.1 %collective-permute-start.31 = (bf16[128,128]{1,0:T(8,128)(2,1)S(1)}, bf16[128,128]{1,0:T(8,128)(2,1)S(1)}, u32[]{:S(2)}, u32[]{:S(2)}) collective-permute-start(bf16[128,128]{1,0:T(8,128)(2,1)S(1)} %get-tuple-element.8), channel_id=1, source_target_pairs={{8,0},{16,8},{24,16},{32,24},{40,32},{48,40},{56,48},{64,56},{72,6... | collective-permute-start | bytes 98312 | tf_op jit(solution)/shard_map/ppermute | solution.py:14
  315.2 8.1 %collective-permute-start.27 = (bf16[128,128]{1,0:T(8,128)(2,1)S(1)}, bf16[128,128]{1,0:T(8,128)(2,1)S(1)}, u32[]{:S(2)}, u32[]{:S(2)}) collective-permute-start(bf16[128,128]{1,0:T(8,128)(2,1)S(1)} %get-tuple-element.11), channel_id=1, source_target_pairs={{0,8},{8,16},{16,24},{24,32},{32,40},{40,48},{48,56},{56,64},{64,7... | collective-permute-start | bytes 98312 | tf_op jit(solution)/shard_map/ppermute | solution.py:14
  317.8 7.9 %collective-permute-start.26 = (bf16[128,128]{1,0:T(8,128)(2,1)S(1)}, bf16[128,128]{1,0:T(8,128)(2,1)S(1)}, u32[]{:S(2)}, u32[]{:S(2)}) collective-permute-start(bf16[128,128]{1,0:T(8,128)(2,1)S(1)} %get-tuple-element.12), channel_id=1, source_target_pairs={{0,8},{8,16},{16,24},{24,32},{32,40},{40,48},{48,56},{56,64},{64,7... | collective-permute-start | bytes 98312 | tf_op jit(solution)/shard_map/ppermute | solution.py:14
  323.3 11.9 %collective-permute-start.30 = (bf16[128,128]{1,0:T(8,128)(2,1)S(1)}, bf16[128,128]{1,0:T(8,128)(2,1)S(1)}, u32[]{:S(2)}, u32[]{:S(2)}) collective-permute-start(bf16[128,128]{1,0:T(8,128)(2,1)S(1)} %get-tuple-element.9), channel_id=1, source_target_pairs={{1,0},{2,1},{3,2},{4,3},{5,4},{6,5},{7,6},{9,8},{10,9},{11,10},{12... | collective-permute-start | bytes 98312 | tf_op jit(solution)/shard_map/ppermute | solution.py:14
  325.7 5.7 %collective-permute-start.28 = (bf16[128,128]{1,0:T(8,128)(2,1)S(1)}, bf16[128,128]{1,0:T(8,128)(2,1)S(1)}, u32[]{:S(2)}, u32[]{:S(2)}) collective-permute-start(bf16[128,128]{1,0:T(8,128)(2,1)S(1)} %collective-permute-done.27), channel_id=1, source_target_pairs={{1,0},{2,1},{3,2},{4,3},{5,4},{6,5},{7,6},{9,8},{10,9},{11,10},{12... | collective-permute-start | bytes 98312 | tf_op jit(solution)/shard_map/ppermute | solution.py:14
  327.1 8.2 %collective-permute-start.29 = (bf16[128,128]{1,0:T(8,128)(2,1)S(1)}, bf16[128,128]{1,0:T(8,128)(2,1)S(1)}, u32[]{:S(2)}, u32[]{:S(2)}) collective-permute-start(bf16[128,128]{1,0:T(8,128)(2,1)S(1)} %get-tuple-element.10), channel_id=1, source_target_pairs={{0,1},{1,2},{2,3},{3,4},{4,5},{5,6},{6,7},{8,9},{9,10},{10,11},{11... | collective-permute-start | bytes 98312 | tf_op jit(solution)/shard_map/ppermute | solution.py:14
  330.1 6.0 %collective-permute-start.35 = (bf16[128,128]{1,0:T(8,128)(2,1)S(1)}, bf16[128,128]{1,0:T(8,128)(2,1)S(1)}, u32[]{:S(2)}, u32[]{:S(2)}) collective-permute-start(bf16[128,128]{1,0:T(8,128)(2,1)S(1)} %collective-permute-done.34), channel_id=1, source_target_pairs={{1,0},{2,1},{3,2},{4,3},{5,4},{6,5},{7,6},{9,8},{10,9},{11,10},{12... | collective-permute-start | bytes 98312 | tf_op jit(solution)/shard_map/ppermute | solution.py:14
  331.4 4.6 %collective-permute-start.32 = (bf16[128,128]{1,0:T(8,128)(2,1)S(1)}, bf16[128,128]{1,0:T(8,128)(2,1)S(1)}, u32[]{:S(2)}, u32[]{:S(2)}) collective-permute-start(bf16[128,128]{1,0:T(8,128)(2,1)S(1)} %collective-permute-done.31), channel_id=1, source_target_pairs={{0,1},{1,2},{2,3},{3,4},{4,5},{5,6},{6,7},{8,9},{9,10},{10,11},{11... | collective-permute-start | bytes 98312 | tf_op jit(solution)/shard_map/ppermute | solution.py:14
Sparse Core Ops, SparseCore 0:
  115.8 33.4 reduce-scatter.9
  254.0 31.7 reduce-scatter.11
  390.1 31.7 reduce-scatter.13
where the time goes:
time: 432 us; the launch traced here: 430 us
  blocking collectives  143 us (33%)
  waiting for transfers between devices  125 us (29%)
  starting transfers between devices  92.6 us (21%)
  matrix products  31.9 us (7%)
  local copies, waits for them, and re-layouts  19.3 us (4%)
  between operations  14.6 us (3%)
  other arithmetic  4.39 us (1%)
    all_gather x3, blocking collectives, local(): lax.all_gather(coarse_rhs, 'sub', axis=0, tiled=True)  143 us
    unnamed x6, waiting for transfers between devices  96.2 us
    ppermute x36, starting transfers between devices, from_behind(): return lax.ppermute(value, axis, pairs)  92.3 us
    ppermute x36, waiting for transfers between devices, from_behind(): return lax.ppermute(value, axis, pairs)  28.5 us
    dot_general x3, matrix products, local(): jnp.dot(inverse, mixed_trace, preferred_element_type=jnp.float32)  21 us
    unnamed x40, local copies, waits for them, and re-layouts  9.05 us
  transfers between devices with their start and end apart: 39, of which 14 were waited for; matrix products, arithmetic and copies ran while one was open for 1% of the time, Pallas kernels for 0%

commit v1 on v0

--- a/solution.py
+++ b/solution.py
@@ -6,6 +6,28 @@
 MODES = 64
 ITERS = 3
 DIRECTIONS = ((-1, -1), (-1, 0), (-1, 1), (0, -1), (0, 1), (1, -1), (1, 0), (1, 1))
+
+
+def joined_along(blocks, dim):
+    shape = list(blocks.shape[1:])
+    shape[dim] *= blocks.shape[0]
+    return jnp.moveaxis(blocks, 0, dim).reshape(shape)
+
+
+def doubled(array, axis):
+    size = lax.axis_size(axis)
+    tiles = array[None]
+    for level in range(size.bit_length() - 1):
+        bit = 1 << level
+        partner_block = lax.ppermute(tiles, axis, [(i, i ^ bit) for i in range(size)])
+        both = jnp.stack([tiles, partner_block])
+        upper = lax.axis_index(axis) >> level & 1
+        tiles = jnp.where(upper == 0, both, both[::-1]).reshape(-1, *array.shape)
+    return tiles
+
+
+def doubled_up(x, axis, dim):
+    return joined_along(doubled(x, axis), dim)
 
 
 def from_behind(value, axis, by):
@@ -80,9 +102,7 @@
             jnp.bfloat16
         )
         partial_value = jnp.dot(
-            coarse_inverse,
-            lax.all_gather(coarse_rhs, "sub", axis=0, tiled=True),
-            preferred_element_type=jnp.float32,
+            coarse_inverse, doubled_up(coarse_rhs, "sub", 0), preferred_element_type=jnp.float32
         )
         coarse_out = lax.psum_scatter(
             partial_value.astype(jnp.bfloat16), "col", scatter_dimension=0, tiled=True

time: 432 us -> 384 us (0.89)
  blocking collectives: 143 us -> 0 us
  waiting for transfers between devices: 125 us -> 205 us
  starting transfers between devices: 92.6 us -> 107 us
    all_gather x3 -> x0, blocking collectives: 143 us -> none  [local(): lax.all_gather(coarse_rhs, 'sub', axis=0, tiled=True)]
    ppermute x0 -> x15, waiting for transfers between devices: none -> 78.4 us  [doubled(): lax.ppermute(tiles, axis, [(i, i ^ bit) for i in range(size)])]
    ppermute x0 -> x15, starting transfers between devices: none -> 14.6 us  [doubled(): lax.ppermute(tiles, axis, [(i, i ^ bit) for i in range(size)])]
  transfers between devices with their start and end apart: 39 -> 54, of which waited for: 14 -> 29; matrix products, arithmetic and copies ran while one was open for 1% -> 1% of each run, Pallas kernels for 0% -> 0%
where the time goes in v1:
time: 384 us; the launch traced here: 382 us
  waiting for transfers between devices  205 us (53%)
  starting transfers between devices  107 us (28%)
  matrix products  31.9 us (8%)
  local copies, waits for them, and re-layouts  18.5 us (5%)
  between operations  14.8 us (4%)
  other arithmetic  5.47 us (1%)
    unnamed x6, waiting for transfers between devices  97.7 us
    ppermute x36, starting transfers between devices, from_behind(): return lax.ppermute(value, axis, pairs)  92.2 us
    ppermute x15, waiting for transfers between devices, doubled(): lax.ppermute(tiles, axis, [(i, i ^ bit) for i in range(size)])  78.4 us
    ppermute x36, waiting for transfers between devices, from_behind(): return lax.ppermute(value, axis, pairs)  28.6 us
    dot_general x3, matrix products, local(): jnp.dot(inverse, mixed_trace, preferred_element_type=jnp.float32)  21 us
    ppermute x15, starting transfers between devices, doubled(): lax.ppermute(tiles, axis, [(i, i ^ bit) for i in range(size)])  14.6 us
    unnamed x40, local copies, waits for them, and re-layouts  8.32 us
  transfers between devices with their start and end apart: 54, of which 29 were waited for; matrix products, arithmetic and copies ran while one was open for 1% of the time, Pallas kernels for 0%

profile of v1, /device:TPU:2, one launch (start us, length us, event | category | flops | bytes accessed | tf_op | source)
XLA Modules:
  0.0 382.2 jit_solution(10032373875493266310)
XLA Ops:
  7.2 1.3 copy.29
  8.6 7.1 %fusion.54 = bf16[1536,128]{0,1:T(8,128)(2,1)S(1)} fusion(bf16[1,1,1536,1536]{3,2,1,0:T(8,128)(2,1)} %param.11, bf16[1,1,1536,1536]{3,2,1,0:T(8,128)(2,1)} %param.10, bf16[1,1,1536,128]{3,2,1,0:T(8,128)(2,1)} %param.8, bf16[1,1,1536,128]{2,3,1,0:T(8,128)(2,1)S(1)} %copy.29), kind=kOutput, calls=%fused_computation.31 | convolution fusion | flops 1208942592 | bytes 10616832 | tf_op jit(solution)/shard_map/dot_general | solution.py:87
  16.3 3.8 %collective-permute-start = (bf16[128,128]{1,0:T(8,128)(2,1)S(1)}, bf16[128,128]{1,0:T(8,128)(2,1)}, u32[]{:S(2)}, u32[]{:S(2)}) collective-permute-start(bf16[128,128]{1,0:T(8,128)(2,1)S(1)} %get-tuple-element.29), channel_id=1, source_target_pairs={{0,8},{8,16},{16,24},{24,32},{32,40},{40,48},{48,56},{56,64},{64,7... | collective-permute-start | bytes 98312 | tf_op jit(solution)/shard_map/ppermute | solution.py:36
  20.2 5.9 %collective-permute-done = bf16[128,128]{1,0:T(8,128)(2,1)} collective-permute-done((bf16[128,128]{1,0:T(8,128)(2,1)S(1)}, bf16[128,128]{1,0:T(8,128)(2,1)}, u32[]{:S(2)}, u32[]{:S(2)}) %collective-permute-start) | collective-permute-done | bytes 32800 | tf_op jit(solution)/shard_map/ppermute | solution.py:36
  26.1 1.9 collective-permute-start.1
  27.9 3.9 %collective-permute-start.10 = (bf16[128,128]{1,0:T(8,128)(2,1)S(1)}, bf16[128,128]{1,0:T(8,128)(2,1)}, u32[]{:S(2)}, u32[]{:S(2)}) collective-permute-start(bf16[128,128]{1,0:T(8,128)(2,1)S(1)} %get-tuple-element.22), channel_id=1, source_target_pairs={{8,0},{16,8},{24,16},{32,24},{40,32},{48,40},{56,48},{64,56},{72,6... | collective-permute-start | bytes 98312 | tf_op jit(solution)/shard_map/ppermute | solution.py:36
  31.9 2.9 collective-permute-start.9
  34.8 2.9 collective-permute-start.7
  37.7 2.9 collective-permute-start.3
  42.6 2.9 collective-permute-start.2
  47.6 2.9 collective-permute-done.2
  51.8 3.0 collective-permute-start.5
  54.9 1.3 collective-permute-start.11
  56.2 3.8 collective-permute-start.8
  62.1 2.0 copy.55
  66.4 3.7 collective-permute-done.12
  70.3 5.3 %collective-permute-done.13 = bf16[2,64,128]{2,1,0:T(8,128)(2,1)S(1)} collective-permute-done((bf16[2,64,128]{2,1,0:T(8,128)(2,1)S(1)}, bf16[2,64,128]{2,1,0:T(8,128)(2,1)S(1)}, u32[]{:S(2)}, u32[]{:S(2)}) %collective-permute-start.13) | collective-permute-done | bytes 32800 | tf_op jit(solution)/shard_map/ppermute | solution.py:22
  76.6 7.4 %collective-permute-done.14 = bf16[4,64,128]{2,1,0:T(8,128)(2,1)S(1)} collective-permute-done((bf16[4,64,128]{2,1,0:T(8,128)(2,1)S(1)}, bf16[4,64,128]{2,1,0:T(8,128)(2,1)S(1)}, u32[]{:S(2)}, u32[]{:S(2)}) %collective-permute-start.14) | collective-permute-done | bytes 65568 | tf_op jit(solution)/shard_map/ppermute | solution.py:22
  84.2 4.9 %collective-permute-done.15 = bf16[8,64,128]{2,1,0:T(8,128)(2,1)S(1)} collective-permute-done((bf16[8,64,128]{2,1,0:T(8,128)(2,1)S(1)}, bf16[8,64,128]{2,1,0:T(8,128)(2,1)S(1)}, u32[]{:S(2)}, u32[]{:S(2)}) %collective-permute-start.15) | collective-permute-done | bytes 131104 | tf_op jit(solution)/shard_map/ppermute | solution.py:22
  89.2 2.8 collective-permute-start.16
  92.0 5.2 %collective-permute-done.16 = bf16[16,64,128]{2,1,0:T(8,128)(2,1)S(1)} collective-permute-done((bf16[16,64,128]{2,1,0:T(8,128)(2,1)S(1)}, bf16[16,64,128]{2,1,0:T(8,128)(2,1)S(1)}, u32[]{:S(2)}, u32[]{:S(2)}) %collective-permute-start.16) | collective-permute-done | bytes 262176 | tf_op jit(solution)/shard_map/ppermute | solution.py:22
  99.1 34.6 %reduce-scatter.10.cloned.1.call-done = bf16[64,128]{1,0:T(8,128)(2,1)} async-done(((bf16[512,128]{1,0:T(8,128)(2,1)}), bf16[64,128]{1,0:T(8,128)(2,1)}) %reduce-scatter.10.cloned.1.call-update) | async-done | bytes 16400
  133.6 1.3 fusion.27
  134.9 6.9 %fusion.51 = bf16[1536,128]{0,1:T(8,128)(2,1)S(1)} fusion(bf16[1,1,1536,1536]{3,2,1,0:T(8,128)(2,1)} %param.11, bf16[1536,128]{0,1:T(8,128)(2,1)S(1)} %fusion.27, bf16[1,1,1536,1536]{3,2,1,0:T(8,128)(2,1)} %param.10), kind=kOutput, calls=%fused_computation.30 | convolution fusion | flops 1208942592 | bytes 10223616 | tf_op jit(solution)/shard_map/dot_general | solution.py:87
  144.1 3.5 collective-permute-start.17
  147.5 4.5 %collective-permute-done.17 = bf16[128,128]{1,0:T(8,128)(2,1)S(1)} collective-permute-done((bf16[128,128]{1,0:T(8,128)(2,1)S(1)}, bf16[128,128]{1,0:T(8,128)(2,1)S(1)}, u32[]{:S(2)}, u32[]{:S(2)}) %collective-permute-start.17) | collective-permute-done | bytes 32800 | tf_op jit(solution)/shard_map/ppermute | solution.py:36
  153.3 3.0 collective-permute-start.27
  156.3 3.4 collective-permute-start.26
  159.7 3.2 collective-permute-start.24
  162.9 2.6 collective-permute-start.20
  165.5 2.5 collective-permute-start.19
  168.1 3.0 collective-permute-done.20
  174.8 3.0 collective-permute-start.22
  177.8 1.3 collective-permute-start.28
  179.1 3.8 collective-permute-start.25
  184.8 2.0 copy.57
  188.4 3.7 collective-permute-done.29
  192.4 5.3 %collective-permute-done.30 = bf16[2,64,128]{2,1,0:T(8,128)(2,1)S(1)} collective-permute-done((bf16[2,64,128]{2,1,0:T(8,128)(2,1)S(1)}, bf16[2,64,128]{2,1,0:T(8,128)(2,1)S(1)}, u32[]{:S(2)}, u32[]{:S(2)}) %collective-permute-start.30) | collective-permute-done | bytes 32800 | tf_op jit(solution)/shard_map/ppermute | solution.py:22
  198.5 7.6 %collective-permute-done.31 = bf16[4,64,128]{2,1,0:T(8,128)(2,1)S(1)} collective-permute-done((bf16[4,64,128]{2,1,0:T(8,128)(2,1)S(1)}, bf16[4,64,128]{2,1,0:T(8,128)(2,1)S(1)}, u32[]{:S(2)}, u32[]{:S(2)}) %collective-permute-start.31) | collective-permute-done | bytes 65568 | tf_op jit(solution)/shard_map/ppermute | solution.py:22
  206.3 5.0 %collective-permute-done.32 = bf16[8,64,128]{2,1,0:T(8,128)(2,1)S(1)} collective-permute-done((bf16[8,64,128]{2,1,0:T(8,128)(2,1)S(1)}, bf16[8,64,128]{2,1,0:T(8,128)(2,1)S(1)}, u32[]{:S(2)}, u32[]{:S(2)}) %collective-permute-start.32) | collective-permute-done | bytes 131104 | tf_op jit(solution)/shard_map/ppermute | solution.py:22
  211.3 4.1 %collective-permute-start.33 = (bf16[16,64,128]{2,1,0:T(8,128)(2,1)S(1)}, bf16[16,64,128]{2,1,0:T(8,128)(2,1)S(1)}, u32[]{:S(2)}, u32[]{:S(2)}) collective-permute-start(bf16[16,64,128]{2,1,0:T(8,128)(2,1)S(1)} %bitcast.299), channel_id=1, source_target_pairs={{0,128},{8,136},{16,144},{24,152},{32,160},{40,168},{48,176},{56,1... | collective-permute-start | bytes 786440 | tf_op jit(solution)/shard_map/ppermute | solution.py:22
  215.5 4.4 %collective-permute-done.33 = bf16[16,64,128]{2,1,0:T(8,128)(2,1)S(1)} collective-permute-done((bf16[16,64,128]{2,1,0:T(8,128)(2,1)S(1)}, bf16[16,64,128]{2,1,0:T(8,128)(2,1)S(1)}, u32[]{:S(2)}, u32[]{:S(2)}) %collective-permute-start.33) | collective-permute-done | bytes 262176 | tf_op jit(solution)/shard_map/ppermute | solution.py:22
  221.7 32.0 %reduce-scatter.12.cloned.1.call-done = bf16[64,128]{1,0:T(8,128)(2,1)} async-done(((bf16[512,128]{1,0:T(8,128)(2,1)}), bf16[64,128]{1,0:T(8,128)(2,1)}) %reduce-scatter.12.cloned.1.call-update) | async-done | bytes 16400
  253.7 1.3 fusion.28
  255.0 6.9 %fusion.48 = bf16[1536,128]{0,1:T(8,128)(2,1)S(1)} fusion(bf16[1,1,1536,1536]{3,2,1,0:T(8,128)(2,1)} %param.11, bf16[1536,128]{0,1:T(8,128)(2,1)S(1)} %fusion.28, bf16[1,1,1536,1536]{3,2,1,0:T(8,128)(2,1)} %param.10), kind=kOutput, calls=%fused_computation.29 | convolution fusion | flops 1208942592 | bytes 10223616 | tf_op jit(solution)/shard_map/dot_general | solution.py:87
  264.3 3.5 collective-permute-start.34
  267.7 4.4 %collective-permute-done.34 = bf16[128,128]{1,0:T(8,128)(2,1)S(1)} collective-permute-done((bf16[128,128]{1,0:T(8,128)(2,1)S(1)}, bf16[128,128]{1,0:T(8,128)(2,1)S(1)}, u32[]{:S(2)}, u32[]{:S(2)}) %collective-permute-start.34) | collective-permute-done | bytes 32800 | tf_op jit(solution)/shard_map/ppermute | solution.py:36
  273.5 3.0 collective-permute-start.44
  276.5 3.3 collective-permute-start.43
  279.9 3.3 collective-permute-start.41
  283.1 2.6 collective-permute-start.37
  285.7 2.5 collective-permute-start.36
  288.2 3.0 collective-permute-done.37
  295.0 3.0 collective-permute-start.39
  298.0 1.3 collective-permute-start.45
  299.3 3.8 collective-permute-start.42
  305.0 2.0 copy.59
  308.7 3.7 collective-permute-done.46
  312.5 5.3 %collective-permute-done.47 = bf16[2,64,128]{2,1,0:T(8,128)(2,1)S(1)} collective-permute-done((bf16[2,64,128]{2,1,0:T(8,128)(2,1)S(1)}, bf16[2,64,128]{2,1,0:T(8,128)(2,1)S(1)}, u32[]{:S(2)}, u32[]{:S(2)}) %collective-permute-start.47) | collective-permute-done | bytes 32800 | tf_op jit(solution)/shard_map/ppermute | solution.py:22
  318.6 7.6 %collective-permute-done.48 = bf16[4,64,128]{2,1,0:T(8,128)(2,1)S(1)} collective-permute-done((bf16[4,64,128]{2,1,0:T(8,128)(2,1)S(1)}, bf16[4,64,128]{2,1,0:T(8,128)(2,1)S(1)}, u32[]{:S(2)}, u32[]{:S(2)}) %collective-permute-start.48) | collective-permute-done | bytes 65568 | tf_op jit(solution)/shard_map/ppermute | solution.py:22
  326.4 5.0 %collective-permute-done.49 = bf16[8,64,128]{2,1,0:T(8,128)(2,1)S(1)} collective-permute-done((bf16[8,64,128]{2,1,0:T(8,128)(2,1)S(1)}, bf16[8,64,128]{2,1,0:T(8,128)(2,1)S(1)}, u32[]{:S(2)}, u32[]{:S(2)}) %collective-permute-start.49) | collective-permute-done | bytes 131104 | tf_op jit(solution)/shard_map/ppermute | solution.py:22
  331.4 4.1 %collective-permute-start.50 = (bf16[16,64,128]{2,1,0:T(8,128)(2,1)S(1)}, bf16[16,64,128]{2,1,0:T(8,128)(2,1)S(1)}, u32[]{:S(2)}, u32[]{:S(2)}) collective-permute-start(bf16[16,64,128]{2,1,0:T(8,128)(2,1)S(1)} %bitcast.297), channel_id=1, source_target_pairs={{0,128},{8,136},{16,144},{24,152},{32,160},{40,168},{48,176},{56,1... | collective-permute-start | bytes 786440 | tf_op jit(solution)/shard_map/ppermute | solution.py:22
  335.6 4.4 %collective-permute-done.50 = bf16[16,64,128]{2,1,0:T(8,128)(2,1)S(1)} collective-permute-done((bf16[16,64,128]{2,1,0:T(8,128)(2,1)S(1)}, bf16[16,64,128]{2,1,0:T(8,128)(2,1)S(1)}, u32[]{:S(2)}, u32[]{:S(2)}) %collective-permute-start.50) | collective-permute-done | bytes 262176 | tf_op jit(solution)/shard_map/ppermute | solution.py:22
  342.7 31.1 %reduce-scatter.14.cloned.1.call-done = bf16[64,128]{1,0:T(8,128)(2,1)} async-done(((bf16[512,128]{1,0:T(8,128)(2,1)}), bf16[64,128]{1,0:T(8,128)(2,1)}) %reduce-scatter.14.cloned.1.call-update) | async-done | bytes 16400
  (157 shorter events, 43.7 us)
Async XLA Ops:
  7.2 90.2 %copy-start = (bf16[512,2048]{1,0:T(8,128)(2,1)S(1)}, bf16[512,2048]{1,0:T(8,128)(2,1)}, u32[]{:S(2)}) copy-start(bf16[512,2048]{1,0:T(8,128)(2,1)} %param.15) | copy-start | bytes 6291460
  7.2 126.4 %reduce-scatter.10.cloned.1.call-start = ((), (), s32[]{:S(2)}) async-start(), calls=%async_computation.3 | async-start | bytes 147456
  8.5 7.3 %copy-start.5 = (s32[1,1,8,128]{3,2,1,0:T(8,128)S(1)}, s32[1,1,8,128]{3,2,1,0:T(8,128)}, u32[]{:S(2)}) copy-start(s32[1,1,8,128]{3,2,1,0:T(8,128)} %param.12) | copy-start | bytes 12292
  8.6 33.3 %copy-start.4 = (bf16[1,1,1536]{2,1,0:T(2,128)(2,1)S(1)}, bf16[1,1,1536]{2,1,0:T(2,128)(2,1)}, u32[]{:S(2)}) copy-start(bf16[1,1,1536]{2,1,0:T(2,128)(2,1)} %param.14) | copy-start | bytes 9220
  16.3 9.7 %collective-permute-start = (bf16[128,128]{1,0:T(8,128)(2,1)S(1)}, bf16[128,128]{1,0:T(8,128)(2,1)}, u32[]{:S(2)}, u32[]{:S(2)}) collective-permute-start(bf16[128,128]{1,0:T(8,128)(2,1)S(1)} %get-tuple-element.29), channel_id=1, source_target_pairs={{0,8},{8,16},{16,24},{24,32},{32,40},{40,48},{48,56},{56,64},{64,7... | collective-permute-start | bytes 98312 | tf_op jit(solution)/shard_map/ppermute | solution.py:36
  26.1 16.5 %collective-permute-start.1 = (bf16[128,128]{1,0:T(8,128)(2,1)}, bf16[128,128]{1,0:T(8,128)(2,1)}, u32[]{:S(2)}, u32[]{:S(2)}) collective-permute-start(bf16[128,128]{1,0:T(8,128)(2,1)} %collective-permute-done), channel_id=1, source_target_pairs={{0,1},{1,2},{2,3},{3,4},{4,5},{5,6},{6,7},{8,9},{9,10},{10,11},{11... | collective-permute-start | bytes 98312 | tf_op jit(solution)/shard_map/ppermute | solution.py:36
  27.9 23.9 %collective-permute-start.10 = (bf16[128,128]{1,0:T(8,128)(2,1)S(1)}, bf16[128,128]{1,0:T(8,128)(2,1)}, u32[]{:S(2)}, u32[]{:S(2)}) collective-permute-start(bf16[128,128]{1,0:T(8,128)(2,1)S(1)} %get-tuple-element.22), channel_id=1, source_target_pairs={{8,0},{16,8},{24,16},{32,24},{40,32},{48,40},{56,48},{64,56},{72,6... | collective-permute-start | bytes 98312 | tf_op jit(solution)/shard_map/ppermute | solution.py:36
  31.9 29.2 %collective-permute-start.9 = (bf16[128,128]{1,0:T(8,128)(2,1)S(1)}, bf16[128,128]{1,0:T(8,128)(2,1)S(1)}, u32[]{:S(2)}, u32[]{:S(2)}) collective-permute-start(bf16[128,128]{1,0:T(8,128)(2,1)S(1)} %get-tuple-element.23), channel_id=1, source_target_pairs={{8,0},{16,8},{24,16},{32,24},{40,32},{48,40},{56,48},{64,56},{72,6... | collective-permute-start | bytes 98312 | tf_op jit(solution)/shard_map/ppermute | solution.py:36
  34.8 20.1 %collective-permute-start.7 = (bf16[128,128]{1,0:T(8,128)(2,1)S(1)}, bf16[128,128]{1,0:T(8,128)(2,1)}, u32[]{:S(2)}, u32[]{:S(2)}) collective-permute-start(bf16[128,128]{1,0:T(8,128)(2,1)S(1)} %get-tuple-element.24), channel_id=1, source_target_pairs={{8,0},{16,8},{24,16},{32,24},{40,32},{48,40},{56,48},{64,56},{72,6... | collective-permute-start | bytes 98312 | tf_op jit(solution)/shard_map/ppermute | solution.py:36
  37.7 8.6 %collective-permute-start.3 = (bf16[128,128]{1,0:T(8,128)(2,1)S(1)}, bf16[128,128]{1,0:T(8,128)(2,1)}, u32[]{:S(2)}, u32[]{:S(2)}) collective-permute-start(bf16[128,128]{1,0:T(8,128)(2,1)S(1)} %get-tuple-element.27), channel_id=1, source_target_pairs={{0,8},{8,16},{16,24},{24,32},{32,40},{40,48},{48,56},{56,64},{64,7... | collective-permute-start | bytes 98312 | tf_op jit(solution)/shard_map/ppermute | solution.py:36
  42.6 7.9 %collective-permute-start.2 = (bf16[128,128]{1,0:T(8,128)(2,1)S(1)}, bf16[128,128]{1,0:T(8,128)(2,1)S(1)}, u32[]{:S(2)}, u32[]{:S(2)}) collective-permute-start(bf16[128,128]{1,0:T(8,128)(2,1)S(1)} %get-tuple-element.28), channel_id=1, source_target_pairs={{0,8},{8,16},{16,24},{24,32},{32,40},{40,48},{48,56},{56,64},{64,7... | collective-permute-start | bytes 98312 | tf_op jit(solution)/shard_map/ppermute | solution.py:36
  46.3 13.7 %collective-permute-start.6 = (bf16[128,128]{1,0:T(8,128)(2,1)S(1)}, bf16[128,128]{1,0:T(8,128)(2,1)S(1)}, u32[]{:S(2)}, u32[]{:S(2)}) collective-permute-start(bf16[128,128]{1,0:T(8,128)(2,1)S(1)} %get-tuple-element.25), channel_id=1, source_target_pairs={{1,0},{2,1},{3,2},{4,3},{5,4},{6,5},{7,6},{9,8},{10,9},{11,10},{12... | collective-permute-start | bytes 98312 | tf_op jit(solution)/shard_map/ppermute | solution.py:36
  50.5 5.7 %collective-permute-start.4 = (bf16[128,128]{1,0:T(8,128)(2,1)}, bf16[128,128]{1,0:T(8,128)(2,1)S(1)}, u32[]{:S(2)}, u32[]{:S(2)}) collective-permute-start(bf16[128,128]{1,0:T(8,128)(2,1)} %collective-permute-done.3), channel_id=1, source_target_pairs={{1,0},{2,1},{3,2},{4,3},{5,4},{6,5},{7,6},{9,8},{10,9},{11,10},{12... | collective-permute-start | bytes 98312 | tf_op jit(solution)/shard_map/ppermute | solution.py:36
  51.8 8.2 %collective-permute-start.5 = (bf16[128,128]{1,0:T(8,128)(2,1)S(1)}, bf16[128,128]{1,0:T(8,128)(2,1)S(1)}, u32[]{:S(2)}, u32[]{:S(2)}) collective-permute-start(bf16[128,128]{1,0:T(8,128)(2,1)S(1)} %get-tuple-element.26), channel_id=1, source_target_pairs={{0,1},{1,2},{2,3},{3,4},{4,5},{5,6},{6,7},{8,9},{9,10},{10,11},{11... | collective-permute-start | bytes 98312 | tf_op jit(solution)/shard_map/ppermute | solution.py:36
  54.9 6.2 %collective-permute-start.11 = (bf16[128,128]{1,0:T(8,128)(2,1)}, bf16[128,128]{1,0:T(8,128)(2,1)S(1)}, u32[]{:S(2)}, u32[]{:S(2)}) collective-permute-start(bf16[128,128]{1,0:T(8,128)(2,1)} %collective-permute-done.10), channel_id=1, source_target_pairs={{1,0},{2,1},{3,2},{4,3},{5,4},{6,5},{7,6},{9,8},{10,9},{11,10},{12... | collective-permute-start | bytes 98312 | tf_op jit(solution)/shard_map/ppermute | solution.py:36
  56.2 4.8 %collective-permute-start.8 = (bf16[128,128]{1,0:T(8,128)(2,1)}, bf16[128,128]{1,0:T(8,128)(2,1)S(1)}, u32[]{:S(2)}, u32[]{:S(2)}) collective-permute-start(bf16[128,128]{1,0:T(8,128)(2,1)} %collective-permute-done.7), channel_id=1, source_target_pairs={{0,1},{1,2},{2,3},{3,4},{4,5},{5,6},{6,7},{8,9},{9,10},{10,11},{11... | collective-permute-start | bytes 98312 | tf_op jit(solution)/shard_map/ppermute | solution.py:36
  65.3 0.7 copy-start.2
  66.3 3.8 %collective-permute-start.12 = (bf16[1,64,128]{2,1,0:T(8,128)(2,1)S(1)}, bf16[1,64,128]{2,1,0:T(8,128)(2,1)S(1)}, u32[]{:S(2)}, u32[]{:S(2)}) collective-permute-start(bf16[1,64,128]{2,1,0:T(8,128)(2,1)S(1)} %bitcast.325), channel_id=1, source_target_pairs={{0,8},{8,0},{16,24},{24,16},{32,40},{40,32},{48,56},{56,48},{64,72... | collective-permute-start | bytes 49160 | tf_op jit(solution)/shard_map/ppermute | solution.py:22
  70.2 5.4 %collective-permute-start.13 = (bf16[2,64,128]{2,1,0:T(8,128)(2,1)S(1)}, bf16[2,64,128]{2,1,0:T(8,128)(2,1)S(1)}, u32[]{:S(2)}, u32[]{:S(2)}) collective-permute-start(bf16[2,64,128]{2,1,0:T(8,128)(2,1)S(1)} %get-tuple-element.35), channel_id=1, source_target_pairs={{0,16},{8,24},{16,0},{24,8},{32,48},{40,56},{48,32},{56,40},{64,80... | collective-permute-start | bytes 98312 | tf_op jit(solution)/shard_map/ppermute | solution.py:22
  75.6 8.4 %collective-permute-start.14 = (bf16[4,64,128]{2,1,0:T(8,128)(2,1)S(1)}, bf16[4,64,128]{2,1,0:T(8,128)(2,1)S(1)}, u32[]{:S(2)}, u32[]{:S(2)}) collective-permute-start(bf16[4,64,128]{2,1,0:T(8,128)(2,1)S(1)} %bitcast.307), channel_id=1, source_target_pairs={{0,32},{8,40},{16,48},{24,56},{32,0},{40,8},{48,16},{56,24},{64,96... | collective-permute-start | bytes 196616 | tf_op jit(solution)/shard_map/ppermute | solution.py:22
  84.1 5.1 %collective-permute-start.15 = (bf16[8,64,128]{2,1,0:T(8,128)(2,1)S(1)}, bf16[8,64,128]{2,1,0:T(8,128)(2,1)S(1)}, u32[]{:S(2)}, u32[]{:S(2)}) collective-permute-start(bf16[8,64,128]{2,1,0:T(8,128)(2,1)S(1)} %bitcast.301), channel_id=1, source_target_pairs={{0,64},{8,72},{16,80},{24,88},{32,96},{40,104},{48,112},{56,120},{... | collective-permute-start | bytes 393224 | tf_op jit(solution)/shard_map/ppermute | solution.py:22
  89.2 8.0 %collective-permute-start.16 = (bf16[16,64,128]{2,1,0:T(8,128)(2,1)S(1)}, bf16[16,64,128]{2,1,0:T(8,128)(2,1)S(1)}, u32[]{:S(2)}, u32[]{:S(2)}) collective-permute-start(bf16[16,64,128]{2,1,0:T(8,128)(2,1)S(1)} %bitcast.295), channel_id=1, source_target_pairs={{0,128},{8,136},{16,144},{24,152},{32,160},{40,168},{48,176},{56,1... | collective-permute-start | bytes 786440 | tf_op jit(solution)/shard_map/ppermute | solution.py:22
  99.0 154.7 %reduce-scatter.12.cloned.1.call-start = ((), (), s32[]{:S(2)}) async-start(), calls=%async_computation.4 | async-start | bytes 147456
  144.1 7.9 %collective-permute-start.17 = (bf16[128,128]{1,0:T(8,128)(2,1)S(1)}, bf16[128,128]{1,0:T(8,128)(2,1)S(1)}, u32[]{:S(2)}, u32[]{:S(2)}) collective-permute-start(bf16[128,128]{1,0:T(8,128)(2,1)S(1)} %get-tuple-element.21), channel_id=1, source_target_pairs={{0,8},{8,16},{16,24},{24,32},{32,40},{40,48},{48,56},{56,64},{64,7... | collective-permute-start | bytes 98312 | tf_op jit(solution)/shard_map/ppermute | solution.py:36
  152.0 13.5 %collective-permute-start.18 = (bf16[128,128]{1,0:T(8,128)(2,1)S(1)}, bf16[128,128]{1,0:T(8,128)(2,1)S(1)}, u32[]{:S(2)}, u32[]{:S(2)}) collective-permute-start(bf16[128,128]{1,0:T(8,128)(2,1)S(1)} %collective-permute-done.17), channel_id=1, source_target_pairs={{0,1},{1,2},{2,3},{3,4},{4,5},{5,6},{6,7},{8,9},{9,10},{10,11},{11... | collective-permute-start | bytes 98312 | tf_op jit(solution)/shard_map/ppermute | solution.py:36
  153.3 21.5 %collective-permute-start.27 = (bf16[128,128]{1,0:T(8,128)(2,1)S(1)}, bf16[128,128]{1,0:T(8,128)(2,1)S(1)}, u32[]{:S(2)}, u32[]{:S(2)}) collective-permute-start(bf16[128,128]{1,0:T(8,128)(2,1)S(1)} %get-tuple-element.14), channel_id=1, source_target_pairs={{8,0},{16,8},{24,16},{32,24},{40,32},{48,40},{56,48},{64,56},{72,6... | collective-permute-start | bytes 98312 | tf_op jit(solution)/shard_map/ppermute | solution.py:36
  156.3 27.5 %collective-permute-start.26 = (bf16[128,128]{1,0:T(8,128)(2,1)S(1)}, bf16[128,128]{1,0:T(8,128)(2,1)S(1)}, u32[]{:S(2)}, u32[]{:S(2)}) collective-permute-start(bf16[128,128]{1,0:T(8,128)(2,1)S(1)} %get-tuple-element.15), channel_id=1, source_target_pairs={{8,0},{16,8},{24,16},{32,24},{40,32},{48,40},{56,48},{64,56},{72,6... | collective-permute-start | bytes 98312 | tf_op jit(solution)/shard_map/ppermute | solution.py:36
  159.7 18.1 %collective-permute-start.24 = (bf16[128,128]{1,0:T(8,128)(2,1)S(1)}, bf16[128,128]{1,0:T(8,128)(2,1)S(1)}, u32[]{:S(2)}, u32[]{:S(2)}) collective-permute-start(bf16[128,128]{1,0:T(8,128)(2,1)S(1)} %get-tuple-element.16), channel_id=1, source_target_pairs={{8,0},{16,8},{24,16},{32,24},{40,32},{48,40},{56,48},{64,56},{72,6... | collective-permute-start | bytes 98312 | tf_op jit(solution)/shard_map/ppermute | solution.py:36
  162.9 8.1 %collective-permute-start.20 = (bf16[128,128]{1,0:T(8,128)(2,1)S(1)}, bf16[128,128]{1,0:T(8,128)(2,1)S(1)}, u32[]{:S(2)}, u32[]{:S(2)}) collective-permute-start(bf16[128,128]{1,0:T(8,128)(2,1)S(1)} %get-tuple-element.19), channel_id=1, source_target_pairs={{0,8},{8,16},{16,24},{24,32},{32,40},{40,48},{48,56},{56,64},{64,7... | collective-permute-start | bytes 98312 | tf_op jit(solution)/shard_map/ppermute | solution.py:36
  165.5 7.9 %collective-permute-start.19 = (bf16[128,128]{1,0:T(8,128)(2,1)S(1)}, bf16[128,128]{1,0:T(8,128)(2,1)S(1)}, u32[]{:S(2)}, u32[]{:S(2)}) collective-permute-start(bf16[128,128]{1,0:T(8,128)(2,1)S(1)} %get-tuple-element.20), channel_id=1, source_target_pairs={{0,8},{8,16},{16,24},{24,32},{32,40},{40,48},{48,56},{56,64},{64,7... | collective-permute-start | bytes 98312 | tf_op jit(solution)/shard_map/ppermute | solution.py:36
  171.0 11.9 %collective-permute-start.23 = (bf16[128,128]{1,0:T(8,128)(2,1)S(1)}, bf16[128,128]{1,0:T(8,128)(2,1)S(1)}, u32[]{:S(2)}, u32[]{:S(2)}) collective-permute-start(bf16[128,128]{1,0:T(8,128)(2,1)S(1)} %get-tuple-element.17), channel_id=1, source_target_pairs={{1,0},{2,1},{3,2},{4,3},{5,4},{6,5},{7,6},{9,8},{10,9},{11,10},{12... | collective-permute-start | bytes 98312 | tf_op jit(solution)/shard_map/ppermute | solution.py:36
  173.5 5.7 %collective-permute-start.21 = (bf16[128,128]{1,0:T(8,128)(2,1)S(1)}, bf16[128,128]{1,0:T(8,128)(2,1)S(1)}, u32[]{:S(2)}, u32[]{:S(2)}) collective-permute-start(bf16[128,128]{1,0:T(8,128)(2,1)S(1)} %collective-permute-done.20), channel_id=1, source_target_pairs={{1,0},{2,1},{3,2},{4,3},{5,4},{6,5},{7,6},{9,8},{10,9},{11,10},{12... | collective-permute-start | bytes 98312 | tf_op jit(solution)/shard_map/ppermute | solution.py:36
  174.8 8.2 %collective-permute-start.22 = (bf16[128,128]{1,0:T(8,128)(2,1)S(1)}, bf16[128,128]{1,0:T(8,128)(2,1)S(1)}, u32[]{:S(2)}, u32[]{:S(2)}) collective-permute-start(bf16[128,128]{1,0:T(8,128)(2,1)S(1)} %get-tuple-element.18), channel_id=1, source_target_pairs={{0,1},{1,2},{2,3},{3,4},{4,5},{5,6},{6,7},{8,9},{9,10},{10,11},{11... | collective-permute-start | bytes 98312 | tf_op jit(solution)/shard_map/ppermute | solution.py:36
  177.8 6.0 %collective-permute-start.28 = (bf16[128,128]{1,0:T(8,128)(2,1)S(1)}, bf16[128,128]{1,0:T(8,128)(2,1)S(1)}, u32[]{:S(2)}, u32[]{:S(2)}) collective-permute-start(bf16[128,128]{1,0:T(8,128)(2,1)S(1)} %collective-permute-done.27), channel_id=1, source_target_pairs={{1,0},{2,1},{3,2},{4,3},{5,4},{6,5},{7,6},{9,8},{10,9},{11,10},{12... | collective-permute-start | bytes 98312 | tf_op jit(solution)/shard_map/ppermute | solution.py:36
  179.1 4.6 %collective-permute-start.25 = (bf16[128,128]{1,0:T(8,128)(2,1)S(1)}, bf16[128,128]{1,0:T(8,128)(2,1)S(1)}, u32[]{:S(2)}, u32[]{:S(2)}) collective-permute-start(bf16[128,128]{1,0:T(8,128)(2,1)S(1)} %collective-permute-done.24), channel_id=1, source_target_pairs={{0,1},{1,2},{2,3},{3,4},{4,5},{5,6},{6,7},{8,9},{9,10},{10,11},{11... | collective-permute-start | bytes 98312 | tf_op jit(solution)/shard_map/ppermute | solution.py:36
  188.0 32.0 %copy-start.3 = (bf16[1536,128]{0,1:T(8,128)(2,1)}, bf16[1536,128]{0,1:T(8,128)(2,1)S(1)}, u32[]{:S(2)}) copy-start(bf16[1536,128]{0,1:T(8,128)(2,1)S(1)} %fusion.62) | copy-start | bytes 1179652
  188.3 3.8 %collective-permute-start.29 = (bf16[1,64,128]{2,1,0:T(8,128)(2,1)S(1)}, bf16[1,64,128]{2,1,0:T(8,128)(2,1)S(1)}, u32[]{:S(2)}, u32[]{:S(2)}) collective-permute-start(bf16[1,64,128]{2,1,0:T(8,128)(2,1)S(1)} %bitcast.328), channel_id=1, source_target_pairs={{0,8},{8,0},{16,24},{24,16},{32,40},{40,32},{48,56},{56,48},{64,72... | collective-permute-start | bytes 49160 | tf_op jit(solution)/shard_map/ppermute | solution.py:22
  192.2 5.6 %collective-permute-start.30 = (bf16[2,64,128]{2,1,0:T(8,128)(2,1)S(1)}, bf16[2,64,128]{2,1,0:T(8,128)(2,1)S(1)}, u32[]{:S(2)}, u32[]{:S(2)}) collective-permute-start(bf16[2,64,128]{2,1,0:T(8,128)(2,1)S(1)} %get-tuple-element.33), channel_id=1, source_target_pairs={{0,16},{8,24},{16,0},{24,8},{32,48},{40,56},{48,32},{56,40},{64,80... | collective-permute-start | bytes 98312 | tf_op jit(solution)/shard_map/ppermute | solution.py:22
  197.8 8.4 %collective-permute-start.31 = (bf16[4,64,128]{2,1,0:T(8,128)(2,1)S(1)}, bf16[4,64,128]{2,1,0:T(8,128)(2,1)S(1)}, u32[]{:S(2)}, u32[]{:S(2)}) collective-permute-start(bf16[4,64,128]{2,1,0:T(8,128)(2,1)S(1)} %bitcast.311), channel_id=1, source_target_pairs={{0,32},{8,40},{16,48},{24,56},{32,0},{40,8},{48,16},{56,24},{64,96... | collective-permute-start | bytes 196616 | tf_op jit(solution)/shard_map/ppermute | solution.py:22
  206.2 5.1 %collective-permute-start.32 = (bf16[8,64,128]{2,1,0:T(8,128)(2,1)S(1)}, bf16[8,64,128]{2,1,0:T(8,128)(2,1)S(1)}, u32[]{:S(2)}, u32[]{:S(2)}) collective-permute-start(bf16[8,64,128]{2,1,0:T(8,128)(2,1)S(1)} %bitcast.305), channel_id=1, source_target_pairs={{0,64},{8,72},{16,80},{24,88},{32,96},{40,104},{48,112},{56,120},{... | collective-permute-start | bytes 393224 | tf_op jit(solution)/shard_map/ppermute | solution.py:22
  211.3 8.5 %collective-permute-start.33 = (bf16[16,64,128]{2,1,0:T(8,128)(2,1)S(1)}, bf16[16,64,128]{2,1,0:T(8,128)(2,1)S(1)}, u32[]{:S(2)}, u32[]{:S(2)}) collective-permute-start(bf16[16,64,128]{2,1,0:T(8,128)(2,1)S(1)} %bitcast.299), channel_id=1, source_target_pairs={{0,128},{8,136},{16,144},{24,152},{32,160},{40,168},{48,176},{56,1... | collective-permute-start | bytes 786440 | tf_op jit(solution)/shard_map/ppermute | solution.py:22
  221.7 152.1 %reduce-scatter.14.cloned.1.call-start = ((), (), s32[]{:S(2)}) async-start(), calls=%async_computation.5 | async-start | bytes 147456
  261.9 43.1 %copy-start.1 = (bf16[1536,128]{0,1:T(8,128)(2,1)}, bf16[1536,128]{0,1:T(8,128)(2,1)S(1)}, u32[]{:S(2)}) copy-start(bf16[1536,128]{0,1:T(8,128)(2,1)S(1)} %fusion.48) | copy-start | bytes 1179652
  264.3 7.9 %collective-permute-start.34 = (bf16[128,128]{1,0:T(8,128)(2,1)S(1)}, bf16[128,128]{1,0:T(8,128)(2,1)S(1)}, u32[]{:S(2)}, u32[]{:S(2)}) collective-permute-start(bf16[128,128]{1,0:T(8,128)(2,1)S(1)} %get-tuple-element.13), channel_id=1, source_target_pairs={{0,8},{8,16},{16,24},{24,32},{32,40},{40,48},{48,56},{56,64},{64,7... | collective-permute-start | bytes 98312 | tf_op jit(solution)/shard_map/ppermute | solution.py:36
  272.2 13.5 %collective-permute-start.35 = (bf16[128,128]{1,0:T(8,128)(2,1)S(1)}, bf16[128,128]{1,0:T(8,128)(2,1)S(1)}, u32[]{:S(2)}, u32[]{:S(2)}) collective-permute-start(bf16[128,128]{1,0:T(8,128)(2,1)S(1)} %collective-permute-done.34), channel_id=1, source_target_pairs={{0,1},{1,2},{2,3},{3,4},{4,5},{5,6},{6,7},{8,9},{9,10},{10,11},{11... | collective-permute-start | bytes 98312 | tf_op jit(solution)/shard_map/ppermute | solution.py:36
  273.5 21.5 %collective-permute-start.44 = (bf16[128,128]{1,0:T(8,128)(2,1)S(1)}, bf16[128,128]{1,0:T(8,128)(2,1)S(1)}, u32[]{:S(2)}, u32[]{:S(2)}) collective-permute-start(bf16[128,128]{1,0:T(8,128)(2,1)S(1)} %get-tuple-element.6), channel_id=1, source_target_pairs={{8,0},{16,8},{24,16},{32,24},{40,32},{48,40},{56,48},{64,56},{72,6... | collective-permute-start | bytes 98312 | tf_op jit(solution)/shard_map/ppermute | solution.py:36
  276.5 27.4 %collective-permute-start.43 = (bf16[128,128]{1,0:T(8,128)(2,1)S(1)}, bf16[128,128]{1,0:T(8,128)(2,1)S(1)}, u32[]{:S(2)}, u32[]{:S(2)}) collective-permute-start(bf16[128,128]{1,0:T(8,128)(2,1)S(1)} %get-tuple-element.7), channel_id=1, source_target_pairs={{8,0},{16,8},{24,16},{32,24},{40,32},{48,40},{56,48},{64,56},{72,6... | collective-permute-start | bytes 98312 | tf_op jit(solution)/shard_map/ppermute | solution.py:36
  279.9 18.1 %collective-permute-start.41 = (bf16[128,128]{1,0:T(8,128)(2,1)S(1)}, bf16[128,128]{1,0:T(8,128)(2,1)S(1)}, u32[]{:S(2)}, u32[]{:S(2)}) collective-permute-start(bf16[128,128]{1,0:T(8,128)(2,1)S(1)} %get-tuple-element.8), channel_id=1, source_target_pairs={{8,0},{16,8},{24,16},{32,24},{40,32},{48,40},{56,48},{64,56},{72,6... | collective-permute-start | bytes 98312 | tf_op jit(solution)/shard_map/ppermute | solution.py:36
  283.1 8.1 %collective-permute-start.37 = (bf16[128,128]{1,0:T(8,128)(2,1)S(1)}, bf16[128,128]{1,0:T(8,128)(2,1)S(1)}, u32[]{:S(2)}, u32[]{:S(2)}) collective-permute-start(bf16[128,128]{1,0:T(8,128)(2,1)S(1)} %get-tuple-element.11), channel_id=1, source_target_pairs={{0,8},{8,16},{16,24},{24,32},{32,40},{40,48},{48,56},{56,64},{64,7... | collective-permute-start | bytes 98312 | tf_op jit(solution)/shard_map/ppermute | solution.py:36
  285.7 7.9 %collective-permute-start.36 = (bf16[128,128]{1,0:T(8,128)(2,1)S(1)}, bf16[128,128]{1,0:T(8,128)(2,1)S(1)}, u32[]{:S(2)}, u32[]{:S(2)}) collective-permute-start(bf16[128,128]{1,0:T(8,128)(2,1)S(1)} %get-tuple-element.12), channel_id=1, source_target_pairs={{0,8},{8,16},{16,24},{24,32},{32,40},{40,48},{48,56},{56,64},{64,7... | collective-permute-start | bytes 98312 | tf_op jit(solution)/shard_map/ppermute | solution.py:36
  291.2 11.9 %collective-permute-start.40 = (bf16[128,128]{1,0:T(8,128)(2,1)S(1)}, bf16[128,128]{1,0:T(8,128)(2,1)S(1)}, u32[]{:S(2)}, u32[]{:S(2)}) collective-permute-start(bf16[128,128]{1,0:T(8,128)(2,1)S(1)} %get-tuple-element.9), channel_id=1, source_target_pairs={{1,0},{2,1},{3,2},{4,3},{5,4},{6,5},{7,6},{9,8},{10,9},{11,10},{12... | collective-permute-start | bytes 98312 | tf_op jit(solution)/shard_map/ppermute | solution.py:36
  293.6 5.7 %collective-permute-start.38 = (bf16[128,128]{1,0:T(8,128)(2,1)S(1)}, bf16[128,128]{1,0:T(8,128)(2,1)S(1)}, u32[]{:S(2)}, u32[]{:S(2)}) collective-permute-start(bf16[128,128]{1,0:T(8,128)(2,1)S(1)} %collective-permute-done.37), channel_id=1, source_target_pairs={{1,0},{2,1},{3,2},{4,3},{5,4},{6,5},{7,6},{9,8},{10,9},{11,10},{12... | collective-permute-start | bytes 98312 | tf_op jit(solution)/shard_map/ppermute | solution.py:36
  295.0 8.2 %collective-permute-start.39 = (bf16[128,128]{1,0:T(8,128)(2,1)S(1)}, bf16[128,128]{1,0:T(8,128)(2,1)S(1)}, u32[]{:S(2)}, u32[]{:S(2)}) collective-permute-start(bf16[128,128]{1,0:T(8,128)(2,1)S(1)} %get-tuple-element.10), channel_id=1, source_target_pairs={{0,1},{1,2},{2,3},{3,4},{4,5},{5,6},{6,7},{8,9},{9,10},{10,11},{11... | collective-permute-start | bytes 98312 | tf_op jit(solution)/shard_map/ppermute | solution.py:36
  298.0 6.0 %collective-permute-start.45 = (bf16[128,128]{1,0:T(8,128)(2,1)S(1)}, bf16[128,128]{1,0:T(8,128)(2,1)S(1)}, u32[]{:S(2)}, u32[]{:S(2)}) collective-permute-start(bf16[128,128]{1,0:T(8,128)(2,1)S(1)} %collective-permute-done.44), channel_id=1, source_target_pairs={{1,0},{2,1},{3,2},{4,3},{5,4},{6,5},{7,6},{9,8},{10,9},{11,10},{12... | collective-permute-start | bytes 98312 | tf_op jit(solution)/shard_map/ppermute | solution.py:36
  299.3 4.6 %collective-permute-start.42 = (bf16[128,128]{1,0:T(8,128)(2,1)S(1)}, bf16[128,128]{1,0:T(8,128)(2,1)S(1)}, u32[]{:S(2)}, u32[]{:S(2)}) collective-permute-start(bf16[128,128]{1,0:T(8,128)(2,1)S(1)} %collective-permute-done.41), channel_id=1, source_target_pairs={{0,1},{1,2},{2,3},{3,4},{4,5},{5,6},{6,7},{8,9},{9,10},{10,11},{11... | collective-permute-start | bytes 98312 | tf_op jit(solution)/shard_map/ppermute | solution.py:36
  308.6 3.8 %collective-permute-start.46 = (bf16[1,64,128]{2,1,0:T(8,128)(2,1)S(1)}, bf16[1,64,128]{2,1,0:T(8,128)(2,1)S(1)}, u32[]{:S(2)}, u32[]{:S(2)}) collective-permute-start(bf16[1,64,128]{2,1,0:T(8,128)(2,1)S(1)} %bitcast.330), channel_id=1, source_target_pairs={{0,8},{8,0},{16,24},{24,16},{32,40},{40,32},{48,56},{56,48},{64,72... | collective-permute-start | bytes 49160 | tf_op jit(solution)/shard_map/ppermute | solution.py:22
  312.4 5.4 %collective-permute-start.47 = (bf16[2,64,128]{2,1,0:T(8,128)(2,1)S(1)}, bf16[2,64,128]{2,1,0:T(8,128)(2,1)S(1)}, u32[]{:S(2)}, u32[]{:S(2)}) collective-permute-start(bf16[2,64,128]{2,1,0:T(8,128)(2,1)S(1)} %get-tuple-element.31), channel_id=1, source_target_pairs={{0,16},{8,24},{16,0},{24,8},{32,48},{40,56},{48,32},{56,40},{64,80... | collective-permute-start | bytes 98312 | tf_op jit(solution)/shard_map/ppermute | solution.py:22
  317.9 8.4 %collective-permute-start.48 = (bf16[4,64,128]{2,1,0:T(8,128)(2,1)S(1)}, bf16[4,64,128]{2,1,0:T(8,128)(2,1)S(1)}, u32[]{:S(2)}, u32[]{:S(2)}) collective-permute-start(bf16[4,64,128]{2,1,0:T(8,128)(2,1)S(1)} %bitcast.309), channel_id=1, source_target_pairs={{0,32},{8,40},{16,48},{24,56},{32,0},{40,8},{48,16},{56,24},{64,96... | collective-permute-start | bytes 196616 | tf_op jit(solution)/shard_map/ppermute | solution.py:22
  326.3 5.1 %collective-permute-start.49 = (bf16[8,64,128]{2,1,0:T(8,128)(2,1)S(1)}, bf16[8,64,128]{2,1,0:T(8,128)(2,1)S(1)}, u32[]{:S(2)}, u32[]{:S(2)}) collective-permute-start(bf16[8,64,128]{2,1,0:T(8,128)(2,1)S(1)} %bitcast.303), channel_id=1, source_target_pairs={{0,64},{8,72},{16,80},{24,88},{32,96},{40,104},{48,112},{56,120},{... | collective-permute-start | bytes 393224 | tf_op jit(solution)/shard_map/ppermute | solution.py:22
  331.4 8.5 %collective-permute-start.50 = (bf16[16,64,128]{2,1,0:T(8,128)(2,1)S(1)}, bf16[16,64,128]{2,1,0:T(8,128)(2,1)S(1)}, u32[]{:S(2)}, u32[]{:S(2)}) collective-permute-start(bf16[16,64,128]{2,1,0:T(8,128)(2,1)S(1)} %bitcast.297), channel_id=1, source_target_pairs={{0,128},{8,136},{16,144},{24,152},{32,160},{40,168},{48,176},{56,1... | collective-permute-start | bytes 786440 | tf_op jit(solution)/shard_map/ppermute | solution.py:22
Sparse Core Ops, SparseCore 0:
  99.1 34.4 reduce-scatter.9
  221.8 31.8 reduce-scatter.11
  341.9 31.8 reduce-scatter.13
